TPU v7x, 32 devices: a whole 2x2x4 slice. The times are simulated.
32 devices in a mesh: group: 2 (over x), tile: 16 (over z, y, core).
Axes of the slice: x: 2, y: 2, z: 4, core: 2. Of those that a mesh axis runs over, the one named last changes fastest.
Arguments:
- residual: bfloat16 [4096, 128], P(('group', 'tile')), parts along dimension 0, may hold values from -6 to 6
- chosen: int32 [512], P(('group', 'tile')), parts along dimension 0, may hold values 0 or 1
- footprint_tile: int32 [2048, 4], P('tile'), may hold values from 0 to 15, all different within a row; in each aligned block of 128 rows (0 to 127, 128 to 255, ...) at most 32 rows name the same one
- footprint_block: int32 [2048, 4], P('tile'), may hold values from 0 to 6143
- interp: float32 [128, 128], replicated, may hold values from -0.5 to 0.5
- speed: float32 [64, 384, 512], P('tile'), may hold values from 0.25 to 1
Outputs:
- adjoint_field: float32 [128, 384, 512], P(('group', 'tile')), parts along dimension 0
- partials: float32 [4096, 128], P(('group', 'tile')), parts along dimension 0
There are 2 independent parts, one for each index of `group`. A program takes and returns all parts, laid end to end along the dimension named above; an argument that names none is the same for every part. Nothing has to cross between parts.
Inputs may be any that keep to these rules, and one draw needn't show every extreme that they name: `footprint_tile`: the 4 tiles of a row differ; within the rows of one device no tile is named by more than 32 rows, a bound that some block reaches.
All inputs are finite; a program needn't handle non-finite values. No bound on the sum of `chosen` on one device may be relied on, other than what follows from the above.
Results may differ from a plain program's by a relative error of at most 0.0014.
Values may be sent and summed in bfloat16 or wider, within the bound.
A program may use at most 128 MiB of HBM per device.

v0:
```python
import jax
import jax.numpy as jnp
from jax import lax
from jax.sharding import PartitionSpec as P

CAP = 32
STEPS = 4


pseudo_rate = 0.16


def padded_2(block, sides, width):
    for axis, dim in sides:
        count = lax.axis_size(axis)
        forward = [(i, i + 1) for i in range(count - 1)]
        backward = [(target, source) for source, target in forward]
        low = lax.ppermute(
            lax.slice_in_dim(block, block.shape[dim] - width, None, axis=dim), axis, forward
        )
        high = lax.ppermute(lax.slice_in_dim(block, 0, width, axis=dim), axis, backward)
        block = jnp.concatenate([low, block, high], axis=dim)
    return block


def lateral(field):
    padded = jnp.pad(field, ((0, 0), (1, 1), (1, 1)))
    beside = padded[:, 2:, 1:-1] + padded[:, :-2, 1:-1]
    return beside + padded[:, 1:-1, 2:] + padded[:, 1:-1, :-2]


def body(residual, chosen, footprint_tile, footprint_block, interp, speed):
    tiles = lax.axis_size("tile")
    rows_dev, top = footprint_tile.shape
    samp = residual.shape[1]
    cx, ny, nz = speed.shape
    cblk = cx * ny * nz // samp
    slots = tiles * CAP
    keep = jnp.repeat(chosen, rows_dev // chosen.shape[0]).astype(jnp.bfloat16)
    masked = residual * keep[:, None]
    dest = footprint_tile.reshape(-1)
    matches = (dest[:, None] == jnp.arange(tiles, dtype=jnp.int32)[None, :]).astype(jnp.int32)
    ranks = jnp.cumsum(matches, axis=0) - 1
    place = jnp.sum(ranks * matches, axis=1)
    slot_of = dest * CAP + place
    row_of = jnp.arange(rows_dev * top, dtype=jnp.int32) // top
    offsets = footprint_block.reshape(-1)
    upper = jnp.full((slots,), -1, jnp.int32).at[slot_of].set(offsets // 64)
    lower = jnp.zeros((slots,), jnp.int32).at[slot_of].set(offsets % 64)
    codes = jnp.stack([upper.reshape(tiles, CAP), lower.reshape(tiles, CAP)], axis=1)
    payload = jnp.zeros((slots, samp), jnp.bfloat16).at[slot_of].set(masked[row_of])
    got, got_codes = (
        lax.all_to_all(
            payload.reshape(tiles, CAP, samp), "tile", split_axis=0, concat_axis=0, tiled=True
        ),
        lax.all_to_all(codes.astype(jnp.bfloat16), "tile", split_axis=0, concat_axis=0, tiled=True),
    )
    values = jnp.dot(
        got.reshape(-1, samp).astype(jnp.float32), interp, precision=lax.Precision.HIGHEST
    )
    recv_upper = got_codes[:, 0, :].reshape(-1).astype(jnp.int32)
    recv_lower = got_codes[:, 1, :].reshape(-1).astype(jnp.int32)
    valid = recv_upper >= 0
    recv_off = jnp.where(valid, recv_upper * 64 + recv_lower, 0)
    values = jnp.where(valid[:, None], values, 0.0)
    source = jax.ops.segment_sum(values, recv_off, num_segments=cblk)
    field = source.reshape(cx, ny, nz)
    for step in range(STEPS):
        wider = padded_2(field.astype(jnp.bfloat16), (("tile", 0),), 1).astype(field.dtype)
        beside = wider[2:] + wider[:-2] + lateral(field)
        field = field + pseudo_rate * speed * (beside - 6.0 * field)
    blocks = field.reshape(cblk, samp)
    sampled = jnp.dot(blocks[recv_off], interp.T, precision=lax.Precision.HIGHEST)
    sampled = jnp.where(valid[:, None], sampled, 0.0).reshape(tiles, CAP, samp)
    returned = lax.all_to_all(sampled, "tile", split_axis=0, concat_axis=0, tiled=True)
    per_entry = returned.reshape(-1, samp)[slot_of]
    partials = jnp.sum(per_entry.reshape(rows_dev, top, samp), axis=1)
    return (field, partials)


def solution(mesh):
    placed = (
        P(("group", "tile"), None),
        P(("group", "tile")),
        P("tile", None),
        P("tile", None),
        P(),
        P("tile", None, None),
    )
    return jax.shard_map(
        body,
        mesh=mesh,
        in_specs=placed,
        out_specs=(P(("group", "tile"), None, None), P(("group", "tile"), None)),
        check_vma=False,
    )
```

profile of v0, /device:TPU:0, one launch (start us, length us, event | category | flops | bytes accessed | tf_op | source)
XLA Modules:
  0.0 139.8 jit_solution(3206627060638970681)
XLA Ops:
  0.6 0.7 broadcast_multiply_fusion.1
  1.4 0.8 copy.19
  2.6 1.2 reduce-window.6
  4.0 0.8 copy.22
  5.0 2.4 %scatter_custom_fusion = s32[512]{0:T(512)S(1)} fusion(s32[512]{0:T(512)S(1)} %bitcast.36, s32[512]{0:T(512)S(1)} %get-tuple-element.18, s32[]{:T(128)} %constant.54.clone.1), kind=kCustom, calls=%fused_computation.102 | custom fusion | bytes 2052 | tf_op jit(solution)/shard_map/scatter | solution.py:48
  7.5 2.4 %scatter_custom_fusion.1 = s32[512]{0:T(512)S(1)} fusion(s32[512]{0:T(512)S(1)} %bitcast.37, s32[512]{0:T(512)S(1)} %get-tuple-element.19, s32[]{:T(128)} %constant.56.clone.1), kind=kCustom, calls=%fused_computation.98 | custom fusion | bytes 2052 | tf_op jit(solution)/shard_map/scatter | solution.py:49
  10.1 0.6 copy.23
  10.7 7.4 %all-to-all-start = ((bf16[16,2,32]{2,1,0:T(2,128)(2,1)}), bf16[16,2,32]{2,1,0:T(2,128)(2,1)S(1)}, u32[]{:S(2)}, u32[]{:S(2)}) async-start(bf16[16,2,32]{2,1,0:T(2,128)(2,1)} %copy.23), calls=%async_computation | async-start | bytes 16384 | tf_op jit(solution)/shard_map/all_to_all | solution.py:56
  18.2 0.7 convert_element_type.84
  19.0 0.8 broadcast_multiply_fusion
  19.9 3.6 %scatter_custom_fusion.2 = bf16[512,128]{1,0:T(8,128)(2,1)} fusion(s32[512]{0:T(512)S(1)} %bitcast.38, bf16[128,128]{1,0:T(8,128)(2,1)S(1)} %broadcast_multiply_fusion, s32[1024]{0:T(1024)S(1)} %pad_clamp_fusion.2, bf16[]{:T(256)} %constant.62.clone.1), kind=kCustom, calls=%fused_computation.63 | custom fusion | bytes 131074 | tf_op jit(solution)/shard_map/scatter | solution.py:51
  23.5 1.1 all-to-all-done
  24.5 5.0 %all-to-all-start.1 = ((bf16[16,32,128]{2,1,0:T(8,128)(2,1)}), bf16[16,32,128]{2,1,0:T(8,128)(2,1)S(1)}, u32[]{:S(2)}, u32[]{:S(2)}) async-start(bf16[16,32,128]{2,1,0:T(8,128)(2,1)} %bitcast.4), calls=%async_computation.1 | async-start | bytes 262144 | tf_op jit(solution)/shard_map/all_to_all | solution.py:53
  29.6 0.5 broadcast.257
  30.1 0.7 fusion.48
  30.9 6.5 %all-to-all-done.1 = bf16[16,32,128]{2,1,0:T(8,128)(2,1)S(1)} async-done(((bf16[16,32,128]{2,1,0:T(8,128)(2,1)}), bf16[16,32,128]{2,1,0:T(8,128)(2,1)S(1)}, u32[]{:S(2)}, u32[]{:S(2)}) %all-to-all-start.1) | async-done | bytes 131104 | tf_op jit(solution)/shard_map/all_to_all | solution.py:53
  37.7 4.1 %scatter_custom_fusion.3 = f32[6144,128]{1,0:T(8,128)} fusion(s32[512]{0:T(512)S(1)} %reshape.249, f32[512,128]{1,0:T(8,128)S(1)} %convolution_select_fusion.1, f32[]{:T(128)} %constant.53.clone.1), kind=kCustom, calls=%fused_computation.59 | custom fusion | flops 65536 | bytes 3145732 | tf_op jit(solution)/shard_map/scatter-add | solution.py:66
  41.7 2.9 %reshape.194 = f32[4,384,512]{2,1,0:T(8,128)S(1)} reshape(f32[6144,128]{1,0:T(8,128)} %scatter_custom_fusion.3) | data formatting | bytes 6291456 | tf_op jit(solution)/shard_map/reshape | solution.py:67
  44.9 1.4 copy-done.2
  46.3 1.3 collective-permute-start
  47.6 1.6 %collective-permute-start.1 = (bf16[1,384,512]{2,1,0:T(8,128)(2,1)S(1)}, bf16[1,384,512]{2,1,0:T(8,128)(2,1)S(1)}, u32[]{:S(2)}, u32[]{:S(2)}) collective-permute-start(bf16[1,384,512]{2,1,0:T(8,128)(2,1)S(1)} %get-tuple-element.17), channel_id=1, source_target_pairs={{1,0},{2,1},{3,2},{4,3},{5,4},{6,5},{7,6},{8,7},{9,8},{10,9},{11,1... | collective-permute-start | bytes 1179656 | tf_op jit(solution)/shard_map/ppermute | solution.py:21
  49.2 2.3 %collective-permute-done.1 = bf16[1,384,512]{2,1,0:T(8,128)(2,1)S(1)} collective-permute-done((bf16[1,384,512]{2,1,0:T(8,128)(2,1)S(1)}, bf16[1,384,512]{2,1,0:T(8,128)(2,1)S(1)}, u32[]{:S(2)}, u32[]{:S(2)}) %collective-permute-start.1) | collective-permute-done | bytes 393248 | tf_op jit(solution)/shard_map/ppermute | solution.py:21
  51.5 0.4 maximum_convert_fusion
  51.9 3.6 %fusion.46 = (bf16[4,384,512]{2,1,0:T(8,128)(2,1)S(1)}, f32[4,384,512]{2,1,0:T(8,128)S(1)}) fusion(f32[4,384,512]{2,1,0:T(8,128)S(1)} %copy-done.3, f32[6,384,512]{2,1,0:T(8,128)S(1)} %maximum_convert_fusion, f32[4,384,512]{2,1,0:T(8,128)S(1)} %copy-done.1), kind=kLoop, calls=%fused_computation.106 | loop fusion | flops 8650752 | bytes 17301504 | tf_op jit(solution)/shard_map/convert_element_type | solution.py:69
  55.6 7.5 %collective-permute-start.2 = (bf16[1,384,512]{2,1,0:T(8,128)(2,1)S(1)}, bf16[1,384,512]{2,1,0:T(8,128)(2,1)S(1)}, u32[]{:S(2)}, u32[]{:S(2)}) collective-permute-start(bf16[1,384,512]{2,1,0:T(8,128)(2,1)S(1)} %get-tuple-element.14), channel_id=1, source_target_pairs={{0,1},{1,2},{2,3},{3,4},{4,5},{5,6},{6,7},{7,8},{8,9},{9,10},{10,1... | collective-permute-start | bytes 1179656 | tf_op jit(solution)/shard_map/ppermute | solution.py:18
  63.1 1.5 %collective-permute-start.3 = (bf16[1,384,512]{2,1,0:T(8,128)(2,1)S(1)}, bf16[1,384,512]{2,1,0:T(8,128)(2,1)S(1)}, u32[]{:S(2)}, u32[]{:S(2)}) collective-permute-start(bf16[1,384,512]{2,1,0:T(8,128)(2,1)S(1)} %get-tuple-element.15), channel_id=1, source_target_pairs={{1,0},{2,1},{3,2},{4,3},{5,4},{6,5},{7,6},{8,7},{9,8},{10,9},{11,1... | collective-permute-start | bytes 1179656 | tf_op jit(solution)/shard_map/ppermute | solution.py:21
  64.6 2.1 %collective-permute-done.3 = bf16[1,384,512]{2,1,0:T(8,128)(2,1)S(1)} collective-permute-done((bf16[1,384,512]{2,1,0:T(8,128)(2,1)S(1)}, bf16[1,384,512]{2,1,0:T(8,128)(2,1)S(1)}, u32[]{:S(2)}, u32[]{:S(2)}) %collective-permute-start.3) | collective-permute-done | bytes 393248 | tf_op jit(solution)/shard_map/ppermute | solution.py:21
  66.7 0.4 maximum_convert_fusion.1
  67.1 3.6 %fusion.44 = (bf16[4,384,512]{2,1,0:T(8,128)(2,1)S(1)}, f32[4,384,512]{2,1,0:T(8,128)S(1)}) fusion(f32[4,384,512]{2,1,0:T(8,128)S(1)} %get-tuple-element.7, f32[6,384,512]{2,1,0:T(8,128)S(1)} %maximum_convert_fusion.1, f32[4,384,512]{2,1,0:T(8,128)S(1)} %copy-done.1), kind=kLoop, calls=%fused_computation.105 | loop fusion | flops 8650752 | bytes 17301504 | tf_op jit(solution)/shard_map/convert_element_type | solution.py:69
  70.7 8.1 %collective-permute-start.4 = (bf16[1,384,512]{2,1,0:T(8,128)(2,1)S(1)}, bf16[1,384,512]{2,1,0:T(8,128)(2,1)S(1)}, u32[]{:S(2)}, u32[]{:S(2)}) collective-permute-start(bf16[1,384,512]{2,1,0:T(8,128)(2,1)S(1)} %get-tuple-element.12), channel_id=1, source_target_pairs={{0,1},{1,2},{2,3},{3,4},{4,5},{5,6},{6,7},{7,8},{8,9},{9,10},{10,1... | collective-permute-start | bytes 1179656 | tf_op jit(solution)/shard_map/ppermute | solution.py:18
  78.9 1.3 collective-permute-start.5
  80.2 2.3 %collective-permute-done.5 = bf16[1,384,512]{2,1,0:T(8,128)(2,1)S(1)} collective-permute-done((bf16[1,384,512]{2,1,0:T(8,128)(2,1)S(1)}, bf16[1,384,512]{2,1,0:T(8,128)(2,1)S(1)}, u32[]{:S(2)}, u32[]{:S(2)}) %collective-permute-start.5) | collective-permute-done | bytes 393248 | tf_op jit(solution)/shard_map/ppermute | solution.py:21
  82.5 0.4 maximum_convert_fusion.2
  82.9 4.8 %fusion.42 = (bf16[4,384,512]{2,1,0:T(8,128)(2,1)S(1)}, f32[4,384,512]{2,1,0:T(8,128)}) fusion(f32[4,384,512]{2,1,0:T(8,128)S(1)} %get-tuple-element.5, f32[6,384,512]{2,1,0:T(8,128)S(1)} %maximum_convert_fusion.2, f32[4,384,512]{2,1,0:T(8,128)S(1)} %copy-done.1), kind=kLoop, calls=%fused_computation.104 | loop fusion | flops 8650752 | bytes 17301504 | tf_op jit(solution)/shard_map/convert_element_type | solution.py:69
  87.7 1.2 copy-done.5
  88.8 0.9 fusion.49
  89.8 9.0 %collective-permute-start.6 = (bf16[1,384,512]{2,1,0:T(8,128)(2,1)}, bf16[1,384,512]{2,1,0:T(8,128)(2,1)}, u32[]{:S(2)}, u32[]{:S(2)}) collective-permute-start(bf16[1,384,512]{2,1,0:T(8,128)(2,1)} %get-tuple-element.10), channel_id=1, source_target_pairs={{0,1},{1,2},{2,3},{3,4},{4,5},{5,6},{6,7},{7,8},{8,9},{9,10},{10,1... | collective-permute-start | bytes 1179656 | tf_op jit(solution)/shard_map/ppermute | solution.py:18
  98.8 1.3 collective-permute-start.7
  100.2 2.5 %collective-permute-done.7 = bf16[1,384,512]{2,1,0:T(8,128)(2,1)} collective-permute-done((bf16[1,384,512]{2,1,0:T(8,128)(2,1)}, bf16[1,384,512]{2,1,0:T(8,128)(2,1)}, u32[]{:S(2)}, u32[]{:S(2)}) %collective-permute-start.7) | collective-permute-done | bytes 393248 | tf_op jit(solution)/shard_map/ppermute | solution.py:21
  102.8 2.0 %maximum_convert_fusion.3 = f32[6,384,512]{2,1,0:T(8,128)S(1)} fusion(bf16[1,384,512]{2,1,0:T(8,128)(2,1)} %collective-permute-done.7, bf16[4,384,512]{2,1,0:T(8,128)(2,1)} %copy-done.5, bf16[1,384,512]{2,1,0:T(8,128)(2,1)} %collective-permute-done.6), kind=kLoop, calls=%fused_computation.58 | loop fusion | flops 3538944 | bytes 7077888 | tf_op jit(solution)/shard_map/convert_element_type | solution.py:69
  104.8 4.1 %fusion.27 = f32[4,384,512]{2,1,0:T(8,128)} fusion(f32[4,384,512]{2,1,0:T(8,128)S(1)} %copy-done.4, f32[6,384,512]{2,1,0:T(8,128)S(1)} %maximum_convert_fusion.3, f32[4,384,512]{2,1,0:T(8,128)S(1)} %copy-done.1), kind=kLoop, calls=%fused_computation.50 | loop fusion | flops 7864320 | bytes 15728640 | tf_op jit(solution)/shard_map/add | solution.py:71
  108.9 2.7 %reshape.195 = f32[6144,128]{1,0:T(8,128)S(1)} reshape(f32[4,384,512]{2,1,0:T(8,128)} %fusion.27) | data formatting | bytes 6291456 | tf_op jit(solution)/shard_map/reshape | solution.py:72
  111.5 1.0 gather_fusion
  112.6 1.1 convolution_select_fusion
  113.6 14.3 %all-to-all-start.2 = ((f32[16,32,128]{2,1,0:T(8,128)}), f32[16,32,128]{2,1,0:T(8,128)S(1)}, u32[]{:S(2)}, u32[]{:S(2)}) async-start(f32[16,32,128]{2,1,0:T(8,128)} %bitcast.7), calls=%async_computation.2 | async-start | bytes 524288 | tf_op jit(solution)/shard_map/all_to_all | solution.py:75
  128.0 10.0 %all-to-all-done.2 = f32[16,32,128]{2,1,0:T(8,128)S(1)} async-done(((f32[16,32,128]{2,1,0:T(8,128)}), f32[16,32,128]{2,1,0:T(8,128)S(1)}, u32[]{:S(2)}, u32[]{:S(2)}) %all-to-all-start.2) | async-done | bytes 262176 | tf_op jit(solution)/shard_map/all_to_all | solution.py:75
  138.0 1.0 gather_fusion.1
  139.0 0.8 reduce_sum.22
  (47 shorter events, 2.3 us)
Async XLA Ops:
  0.6 36.8 %copy-start = (f32[128,128]{1,0:T(8,128)S(1)}, f32[128,128]{1,0:T(8,128)}, u32[]{:S(2)}) copy-start(f32[128,128]{1,0:T(8,128)} %param.10) | copy-start | bytes 196612
  10.7 13.8 %all-to-all-start = ((bf16[16,2,32]{2,1,0:T(2,128)(2,1)}), bf16[16,2,32]{2,1,0:T(2,128)(2,1)S(1)}, u32[]{:S(2)}, u32[]{:S(2)}) async-start(bf16[16,2,32]{2,1,0:T(2,128)(2,1)} %copy.23), calls=%async_computation | async-start | bytes 16384 | tf_op jit(solution)/shard_map/all_to_all | solution.py:56
  24.5 12.9 %all-to-all-start.1 = ((bf16[16,32,128]{2,1,0:T(8,128)(2,1)}), bf16[16,32,128]{2,1,0:T(8,128)(2,1)S(1)}, u32[]{:S(2)}, u32[]{:S(2)}) async-start(bf16[16,32,128]{2,1,0:T(8,128)(2,1)} %bitcast.4), calls=%async_computation.1 | async-start | bytes 262144 | tf_op jit(solution)/shard_map/all_to_all | solution.py:53
  44.6 1.7 %copy-start.2 = (f32[4,384,512]{2,1,0:T(8,128)}, f32[4,384,512]{2,1,0:T(8,128)S(1)}, u32[]{:S(2)}) copy-start(f32[4,384,512]{2,1,0:T(8,128)S(1)} %reshape.194) | copy-start | bytes 9437188
  46.3 2.9 %collective-permute-start = (bf16[1,384,512]{2,1,0:T(8,128)(2,1)S(1)}, bf16[1,384,512]{2,1,0:T(8,128)(2,1)S(1)}, u32[]{:S(2)}, u32[]{:S(2)}) collective-permute-start(bf16[1,384,512]{2,1,0:T(8,128)(2,1)S(1)} %get-tuple-element.16), channel_id=1, source_target_pairs={{0,1},{1,2},{2,3},{3,4},{4,5},{5,6},{6,7},{7,8},{8,9},{9,10},{10,1... | collective-permute-start | bytes 1179656 | tf_op jit(solution)/shard_map/ppermute | solution.py:18
  47.6 4.3 %copy-start.1 = (f32[4,384,512]{2,1,0:T(8,128)S(1)}, f32[4,384,512]{2,1,0:T(8,128)}, u32[]{:S(2)}) copy-start(f32[4,384,512]{2,1,0:T(8,128)} %param.11) | copy-start | bytes 9437188
  47.6 4.3 %copy-start.3 = (f32[4,384,512]{2,1,0:T(8,128)S(1)}, f32[4,384,512]{2,1,0:T(8,128)}, u32[]{:S(2)}) copy-start(f32[4,384,512]{2,1,0:T(8,128)} %copy-done.2) | copy-start | bytes 9437188
  47.6 3.9 %collective-permute-start.1 = (bf16[1,384,512]{2,1,0:T(8,128)(2,1)S(1)}, bf16[1,384,512]{2,1,0:T(8,128)(2,1)S(1)}, u32[]{:S(2)}, u32[]{:S(2)}) collective-permute-start(bf16[1,384,512]{2,1,0:T(8,128)(2,1)S(1)} %get-tuple-element.17), channel_id=1, source_target_pairs={{1,0},{2,1},{3,2},{4,3},{5,4},{6,5},{7,6},{8,7},{9,8},{10,9},{11,1... | collective-permute-start | bytes 1179656 | tf_op jit(solution)/shard_map/ppermute | solution.py:21
  55.6 9.0 %collective-permute-start.2 = (bf16[1,384,512]{2,1,0:T(8,128)(2,1)S(1)}, bf16[1,384,512]{2,1,0:T(8,128)(2,1)S(1)}, u32[]{:S(2)}, u32[]{:S(2)}) collective-permute-start(bf16[1,384,512]{2,1,0:T(8,128)(2,1)S(1)} %get-tuple-element.14), channel_id=1, source_target_pairs={{0,1},{1,2},{2,3},{3,4},{4,5},{5,6},{6,7},{7,8},{8,9},{9,10},{10,1... | collective-permute-start | bytes 1179656 | tf_op jit(solution)/shard_map/ppermute | solution.py:18
  63.1 3.6 %collective-permute-start.3 = (bf16[1,384,512]{2,1,0:T(8,128)(2,1)S(1)}, bf16[1,384,512]{2,1,0:T(8,128)(2,1)S(1)}, u32[]{:S(2)}, u32[]{:S(2)}) collective-permute-start(bf16[1,384,512]{2,1,0:T(8,128)(2,1)S(1)} %get-tuple-element.15), channel_id=1, source_target_pairs={{1,0},{2,1},{3,2},{4,3},{5,4},{6,5},{7,6},{8,7},{9,8},{10,9},{11,1... | collective-permute-start | bytes 1179656 | tf_op jit(solution)/shard_map/ppermute | solution.py:21
  70.7 9.4 %collective-permute-start.4 = (bf16[1,384,512]{2,1,0:T(8,128)(2,1)S(1)}, bf16[1,384,512]{2,1,0:T(8,128)(2,1)S(1)}, u32[]{:S(2)}, u32[]{:S(2)}) collective-permute-start(bf16[1,384,512]{2,1,0:T(8,128)(2,1)S(1)} %get-tuple-element.12), channel_id=1, source_target_pairs={{0,1},{1,2},{2,3},{3,4},{4,5},{5,6},{6,7},{7,8},{8,9},{9,10},{10,1... | collective-permute-start | bytes 1179656 | tf_op jit(solution)/shard_map/ppermute | solution.py:18
  78.9 3.6 %collective-permute-start.5 = (bf16[1,384,512]{2,1,0:T(8,128)(2,1)S(1)}, bf16[1,384,512]{2,1,0:T(8,128)(2,1)S(1)}, u32[]{:S(2)}, u32[]{:S(2)}) collective-permute-start(bf16[1,384,512]{2,1,0:T(8,128)(2,1)S(1)} %get-tuple-element.13), channel_id=1, source_target_pairs={{1,0},{2,1},{3,2},{4,3},{5,4},{6,5},{7,6},{8,7},{9,8},{10,9},{11,1... | collective-permute-start | bytes 1179656 | tf_op jit(solution)/shard_map/ppermute | solution.py:21
  87.7 1.2 copy-start.5
  89.8 10.4 %collective-permute-start.6 = (bf16[1,384,512]{2,1,0:T(8,128)(2,1)}, bf16[1,384,512]{2,1,0:T(8,128)(2,1)}, u32[]{:S(2)}, u32[]{:S(2)}) collective-permute-start(bf16[1,384,512]{2,1,0:T(8,128)(2,1)} %get-tuple-element.10), channel_id=1, source_target_pairs={{0,1},{1,2},{2,3},{3,4},{4,5},{5,6},{6,7},{7,8},{8,9},{9,10},{10,1... | collective-permute-start | bytes 1179656 | tf_op jit(solution)/shard_map/ppermute | solution.py:18
  98.8 3.9 %collective-permute-start.7 = (bf16[1,384,512]{2,1,0:T(8,128)(2,1)}, bf16[1,384,512]{2,1,0:T(8,128)(2,1)}, u32[]{:S(2)}, u32[]{:S(2)}) collective-permute-start(bf16[1,384,512]{2,1,0:T(8,128)(2,1)} %get-tuple-element.11), channel_id=1, source_target_pairs={{1,0},{2,1},{3,2},{4,3},{5,4},{6,5},{7,6},{8,7},{9,8},{10,9},{11,1... | collective-permute-start | bytes 1179656 | tf_op jit(solution)/shard_map/ppermute | solution.py:21
  100.2 4.5 %copy-start.4 = (f32[4,384,512]{2,1,0:T(8,128)S(1)}, f32[4,384,512]{2,1,0:T(8,128)}, u32[]{:S(2)}) copy-start(f32[4,384,512]{2,1,0:T(8,128)} %get-tuple-element.3) | copy-start | bytes 9437188
  113.6 24.3 %all-to-all-start.2 = ((f32[16,32,128]{2,1,0:T(8,128)}), f32[16,32,128]{2,1,0:T(8,128)S(1)}, u32[]{:S(2)}, u32[]{:S(2)}) async-start(f32[16,32,128]{2,1,0:T(8,128)} %bitcast.7), calls=%async_computation.2 | async-start | bytes 524288 | tf_op jit(solution)/shard_map/all_to_all | solution.py:75
where the time goes:
time: 141 us; the launch traced here: 140 us
  starting transfers between devices  58.3 us (41%)
  other arithmetic  28.6 us (20%)
  waiting for transfers between devices  26.8 us (19%)
  local copies, waits for them, and re-layouts  23.8 us (17%)
    ppermute x4, starting transfers between devices, padded_2(): lax.ppermute(lax.slice_in_dim(block, block.shape[dim] - width, None, axis...  26 us
    all_to_all x1, starting transfers between devices, body(): lax.all_to_all(sampled, 'tile', split_axis=0, concat_axis=0, tiled=True)  14.3 us
    convert_element_type x4, other arithmetic, body(): field.astype(jnp.bfloat16)  12.2 us
    all_to_all x1, waiting for transfers between devices, body(): lax.all_to_all(sampled, 'tile', split_axis=0, concat_axis=0, tiled=True)  10 us
    ppermute x4, waiting for transfers between devices, padded_2(): lax.ppermute(lax.slice_in_dim(block, 0, width, axis=dim), axis, backward)  9.28 us
    all_to_all x1, starting transfers between devices, body(): lax.all_to_all(codes.astype(jnp.bfloat16), 'tile', split_axis=0, concat_a...  7.41 us
    all_to_all x1, waiting for transfers between devices, body(): lax.all_to_all(payload.reshape(tiles, CAP, samp), 'tile', split_axis=0, c...  6.48 us
    ppermute x4, starting transfers between devices, padded_2(): lax.ppermute(lax.slice_in_dim(block, 0, width, axis=dim), axis, backward)  5.6 us
  transfers between devices with their start and end apart: 11, of which 7 were waited for; matrix products, arithmetic and copies ran while one was open for 5% of the time, Pallas kernels for 0%

commit v1 on v0

v1 whole, which is shorter than its diff:
```python
import functools

import jax
import jax.numpy as jnp
from jax import lax
from jax.experimental import pallas as pl
from jax.experimental.pallas import tpu as pltpu
from jax.sharding import PartitionSpec as P

CAP = 32
STEPS = 4
RATE = 0.16
HALO = STEPS - 1
MESH = pl.DeviceIdType.MESH
VMEM = pl.BlockSpec(memory_space=pltpu.VMEM)
SMEM = pl.BlockSpec(memory_space=pltpu.SMEM)
F32 = jnp.float32
BF16 = jnp.bfloat16
HIGH = lax.Precision.HIGHEST


def iota(shape, dim):
    return lax.broadcasted_iota(jnp.int32, shape, dim)


def last_dims(a, b):
    return lax.dot_general(a, b, (((1,), (1,)), ((), ())), preferred_element_type=F32)


def dot32(a, b):
    return lax.dot_general(a, b, (((1,), (0,)), ((), ())), preferred_element_type=F32)


def slot_rows(dest, tiles):
    top, rows = dest.shape
    upper = (iota((rows, rows), 0) < iota((rows, rows), 1)).astype(BF16)
    base = jnp.zeros((tiles, 1), F32)
    out = []
    for k in range(top):
        here = dest[k : k + 1, :]
        hot = (iota((tiles, rows), 0) == here).astype(F32)
        ahead = dot32(hot.astype(BF16), upper) + base
        rank = jnp.sum(hot * ahead, axis=0, keepdims=True).astype(jnp.int32)
        base = base + jnp.sum(hot, axis=1, keepdims=True)
        out.append((hot, rank, here * CAP + rank))
    return out


def pack_kernel(tiles, geom, res_ref, chosen_ref, ft_ref, fb_ref, speed_ref, pay_ref, cod_ref, sp_ref):
    cx, ny, nz = geom
    nzb = nz // 128
    per_layer = ny * nzb
    top, rows = ft_ref.shape
    sensors = chosen_ref.shape[0]
    lane = iota((1, rows), 1)
    keep = jnp.zeros((1, rows), jnp.int32)
    for i in range(sensors):
        keep = jnp.where(lane // (rows // sensors) == i, chosen_ref[i], keep)
    keep = keep.astype(F32)
    block = fb_ref[...]
    layer = jnp.zeros_like(block)
    for i in range(1, cx):
        layer = layer + (block >= i * per_layer).astype(jnp.int32)
    in_layer = block - layer * per_layer
    y = in_layer // nzb
    zb = in_layer - y * nzb
    strip = layer * (ny // 8 + 1) + 1 + y // 8
    flat = (strip * nzb + zb) * 8 + (y - y // 8 * 8)
    hi = (flat // 64).astype(F32)
    lo = (flat - flat // 64 * 64).astype(F32)
    slots = slot_rows(ft_ref[...], tiles)
    place = jnp.zeros((tiles * CAP, rows), F32)
    codes = jnp.zeros((tiles, 128), F32)
    for k, (hot, rank, slot) in enumerate(slots):
        place = place + (iota((tiles * CAP, rows), 0) == slot).astype(F32)
        at = (iota((128, rows), 0) == rank).astype(BF16)
        upper = last_dims((hot * hi[k : k + 1]).astype(BF16), at)
        lower = last_dims((hot * lo[k : k + 1]).astype(BF16), at)
        codes = codes + upper * 64.0 + lower
    payload = dot32((place * keep).astype(BF16), res_ref[...]).astype(BF16)
    pay_ref[0] = jnp.zeros((CAP, 128), BF16)
    pay_ref[tiles + 1] = jnp.zeros((CAP, 128), BF16)
    pay_ref[1 : tiles + 1] = payload.reshape(tiles, CAP, 128)
    codes = codes.astype(jnp.int32)
    cod_ref[0] = jnp.zeros((1, 128), jnp.int32)
    cod_ref[tiles + 1] = jnp.zeros((1, 128), jnp.int32)
    for d in range(tiles):
        cod_ref[1 + d] = codes[d : d + 1]
    for l in range(cx):
        sp_ref[l] = speed_ref[l].astype(BF16)


def greet(n, me, partner=None):
    barrier = pltpu.get_barrier_semaphore()

    @pl.loop(1, n)
    def _(i):
        pl.semaphore_signal(barrier, inc=1, device_id={"tile": lax.rem(me + i, n)}, device_id_type=MESH)

    count = n - 1
    if partner is not None:
        pl.semaphore_signal(barrier, inc=1, device_id={"group": partner}, device_id_type=MESH)
        count += 1
    pl.semaphore_wait(barrier, count)


def send_kernel(n, groups, pay, cod, sp, got, gotc, halo, sems, csems, isem, fsem, dsem, lsem):
    me = lax.axis_index("tile")
    paired = groups % 2 == 0
    g = lax.axis_index("group")
    half = lax.rem(g, 2)
    partner = g + 1 - 2 * half if paired else None
    greet(n, me, partner)
    ny = sp.shape[1]
    rows = ny // 2 if paired else ny
    start = half * rows if paired else 0
    odd = lax.rem(me, 2)
    nb = me + 2 * odd - 1
    cb = me + 1 - 2 * odd
    inter = jnp.logical_and(nb >= 0, nb < n)
    window = pl.ds(start, rows)

    def piece(j):
        return pltpu.make_async_remote_copy(
            sp.at[odd + j, window], halo.at[1 - odd, j, window], isem.at[0, j], isem.at[1, j],
            device_id={"tile": nb}, device_id_type=MESH)

    def forward(j):
        return pltpu.make_async_remote_copy(
            halo.at[odd, j, window], halo.at[odd, j, window], fsem.at[0, j], fsem.at[1, j],
            device_id={"group": partner}, device_id_type=MESH)

    inside = pltpu.make_async_remote_copy(
        sp.at[pl.ds(1 - odd, HALO)], halo.at[odd], dsem.at[0], dsem.at[1],
        device_id={"tile": cb}, device_id_type=MESH)

    @pl.when(inter)
    def _():
        for j in range(HALO):
            piece(j).start()

    inside.start()

    def data(i):
        e = lax.rem(me + i, n)
        return pltpu.make_async_remote_copy(
            pay.at[pl.ds(e, 3)], got.at[me], sems.at[0, i], sems.at[1, i],
            device_id={"tile": e}, device_id_type=MESH)

    def code(i):
        e = lax.rem(me + i, n)
        return pltpu.make_async_remote_copy(
            cod.at[pl.ds(e, 3)], gotc.at[me], csems.at[0, i], csems.at[1, i],
            device_id={"tile": e}, device_id_type=MESH)

    @pl.loop(1, n)
    def _(i):
        data(i).start()
        code(i).start()

    own = pltpu.make_async_copy(pay.at[pl.ds(me, 3)], got.at[me], lsem.at[0])
    ownc = pltpu.make_async_copy(cod.at[pl.ds(me, 3)], gotc.at[me], lsem.at[1])
    own.start()
    ownc.start()

    @pl.when(jnp.logical_not(inter))
    def _():
        halo[odd] = jnp.zeros(halo.shape[1:], halo.dtype)

    if paired:
        @pl.when(inter)
        def _():
            for j in range(HALO):
                piece(j).wait_recv()
                forward(j).start()
            for j in range(HALO):
                piece(j).wait_send()
                forward(j).wait()
    else:
        @pl.when(inter)
        def _():
            for j in range(HALO):
                piece(j).wait()

    inside.wait()

    @pl.loop(1, n)
    def _(i):
        data(i).wait()
        code(i).wait()

    own.wait()
    ownc.wait()


def field_kernel(geom, got, codes, interp, speed, halo, field, sampled, ua, ub, vals):
    cx, ny, nz = geom
    nzb = nz // 128
    tile = nzb * 8
    strips = ny // 8
    pitch = strips + 1
    n = got.shape[0]
    span = 3 * CAP
    layers = 3 * cx
    per_tile = cx * pitch * tile
    vals[...] = jnp.dot(got[...].reshape(n * span, 128).astype(F32), interp[...], precision=HIGH)

    zero = jnp.zeros((tile, 128), F32)

    @pl.loop(0, layers * pitch + 1, unroll=4)
    def _(s):
        ua[pl.ds(pl.multiple_of(s * tile, tile), tile)] = zero

    for l in range(layers + 1):
        ub[l * pitch * tile : l * pitch * tile + tile] = zero

    @pl.loop(0, n)
    def _(s):
        for o in range(3):
            for j in range(CAP):
                at = codes[s * 3 + o, j] + o * per_tile
                ua[pl.ds(at, 1)] = ua[pl.ds(at, 1)] + vals[pl.ds(s * span + o * CAP + j, 1)]

    sub = iota((8, 128), 0)
    lane = iota((8, 128), 1)
    first_sub, last_sub = sub == 0, sub == 7
    first_lane, last_lane = lane == 0, lane == 127

    def layer_step(src, dst, l, rate_of, final):
        @pl.loop(0, strips // 2)
        def _(p):
            rates = [rate_of(p, zb) for zb in range(nzb)]
            for h in range(2):
                base = pl.multiple_of((l * pitch + 1 + p * 2 + h) * tile, tile)
                centre = [src[pl.ds(base + zb * 8, 8)] for zb in range(nzb)]
                for zb in range(nzb):
                    c = centre[zb]
                    before = src[pl.ds(base - tile + zb * 8, 8)]
                    after = src[pl.ds(base + tile + zb * 8, 8)]
                    left = centre[zb - 1] if zb > 0 else 0.0
                    right = centre[zb + 1] if zb + 1 < nzb else 0.0
                    total = src[pl.ds(base - pitch * tile + zb * 8, 8)] + src[pl.ds(base + pitch * tile + zb * 8, 8)]
                    total = total + pltpu.roll(jnp.where(last_sub, before, c), 1, 0)
                    total = total + pltpu.roll(jnp.where(first_sub, after, c), 7, 0)
                    total = total + pltpu.roll(jnp.where(last_lane, left, c), 1, 1)
                    total = total + pltpu.roll(jnp.where(first_lane, right, c), 127, 1)
                    new = c + rates[zb][h * 8 : h * 8 + 8] * (total - 6.0 * c)
                    dst[pl.ds(base + zb * 8, 8)] = new
                    if final is not None:
                        field[final, pl.ds(pl.multiple_of(p * 16 + h * 8, 8), 8), zb * 128 : zb * 128 + 128] = new

    def rate_from(ref, index):
        def rate_of(p, zb):
            rows = pl.ds(pl.multiple_of(p * 16, 16), 16)
            return RATE * ref[(*index, rows, slice(zb * 128, zb * 128 + 128))].astype(F32)
        return rate_of

    src, dst = ua, ub
    for step in range(STEPS):
        reach = STEPS - 1 - step
        for l in range(cx - reach, 2 * cx + reach):
            if l < cx:
                rate_of = rate_from(halo, (0, l - (cx - HALO)))
            elif l >= 2 * cx:
                rate_of = rate_from(halo, (1, l - 2 * cx))
            else:
                rate_of = rate_from(speed, (l - cx,))
            layer_step(src, dst, l, rate_of, l - cx if step == STEPS - 1 else None)
        src, dst = dst, src

    @pl.loop(0, n)
    def _(s):
        for j in range(CAP):
            at = codes[s * 3 + 1, j] + per_tile
            sampled[s, pl.ds(j, 1)] = src[pl.ds(at, 1)]


def return_kernel(n, sampled, ft, interp, out, ret, sems, lsem):
    me = lax.axis_index("tile")
    greet(n, me)

    def block(i):
        e = lax.rem(me + i, n)
        return pltpu.make_async_remote_copy(
            sampled.at[e], ret.at[me], sems.at[0, i], sems.at[1, i],
            device_id={"tile": e}, device_id_type=MESH)

    @pl.loop(1, n)
    def _(i):
        block(i).start()

    own = pltpu.make_async_copy(sampled.at[me], ret.at[me], lsem)
    own.start()
    rows = ft.shape[1]
    place = jnp.zeros((n * CAP, rows), F32)
    for hot, rank, slot in slot_rows(ft[...], n):
        place = place + (iota((n * CAP, rows), 0) == slot).astype(F32)
    own.wait()

    @pl.loop(1, n)
    def _(i):
        block(i).wait()

    total = lax.dot_general(
        place, ret[...].reshape(n * CAP, 128), (((0,), (0,)), ((), ())),
        precision=HIGH, preferred_element_type=F32)
    out[...] = lax.dot_general(
        total, interp[...], (((1,), (1,)), ((), ())), precision=HIGH, preferred_element_type=F32)


def body(groups, residual, chosen, footprint_tile, footprint_block, interp, speed):
    n = lax.axis_size("tile")
    cx, ny, nz = geom = speed.shape
    rows, samp = residual.shape
    shape = jax.ShapeDtypeStruct
    ft, fb = footprint_tile.T, footprint_block.T
    pay, cod, sp = pl.pallas_call(
        functools.partial(pack_kernel, n, geom),
        out_shape=(
            shape((n + 2, CAP, samp), BF16),
            shape((n + 2, 1, 128), jnp.int32),
            shape(geom, BF16),
        ),
        in_specs=[VMEM, SMEM, VMEM, VMEM, VMEM],
        out_specs=(VMEM, VMEM, VMEM),
        name="pack",
    )(residual, chosen, ft, fb, speed)
    dma = pltpu.SemaphoreType.DMA
    got, gotc, halo = pl.pallas_call(
        functools.partial(send_kernel, n, groups),
        out_shape=(
            shape((n, 3, CAP, samp), BF16),
            shape((n, 3, 1, 128), jnp.int32),
            shape((2, HALO, ny, nz), BF16),
        ),
        in_specs=[VMEM] * 3,
        out_specs=(VMEM,) * 3,
        scratch_shapes=[
            dma((2, n)), dma((2, n)), dma((2, HALO)), dma((2, HALO)), dma((2,)), dma((2,)),
        ],
        compiler_params=pltpu.CompilerParams(collective_id=0, has_side_effects=True),
        name="exchange",
    )(pay, cod, sp)
    flat = (3 * cx * (ny // 8 + 1) + 1) * (nz // 16)
    field, sampled = pl.pallas_call(
        functools.partial(field_kernel, geom),
        out_shape=(shape(geom, F32), shape((n, CAP, samp), F32)),
        in_specs=[VMEM, SMEM, VMEM, VMEM, VMEM],
        out_specs=(VMEM, VMEM),
        scratch_shapes=[
            pltpu.VMEM((flat, 128), F32), pltpu.VMEM((flat, 128), F32),
            pltpu.VMEM((n * 3 * CAP, 128), F32),
        ],
        name="field",
    )(got, gotc.reshape(n * 3, 128), interp, speed, halo)
    partials = pl.pallas_call(
        functools.partial(return_kernel, n),
        out_shape=shape((rows, samp), F32),
        in_specs=[VMEM] * 3,
        out_specs=VMEM,
        scratch_shapes=[pltpu.VMEM((n, CAP, samp), F32), dma((2, n)), dma],
        compiler_params=pltpu.CompilerParams(collective_id=1, has_side_effects=True),
        name="give_back",
    )(sampled, ft, interp)
    return field, partials


def solution(mesh):
    placed = (
        P(("group", "tile"), None),
        P(("group", "tile")),
        P("tile", None),
        P("tile", None),
        P(),
        P("tile", None, None),
    )
    return jax.shard_map(
        functools.partial(body, mesh.shape["group"]),
        mesh=mesh,
        in_specs=placed,
        out_specs=(P(("group", "tile"), None, None), P(("group", "tile"), None)),
        check_vma=False,
    )
```

time: 141 us -> 121 us (0.86)
  the two profiles are of different devices: /device:TPU:0 before, /device:TPU:5 now
where the time goes in v1:
time: 121 us
  Pallas kernels  119 us (98%)
  local copies, waits for them, and re-layouts  1.47 us (1%)
    pallas_call x1, Pallas kernels, body(): pl.pallas_call(functools.partial(field_kernel, geom), out_shape=(shape(ge...  71.5 us
    pallas_call x1, Pallas kernels, body(): pl.pallas_call(functools.partial(send_kernel, n, groups), out_shape=(shap...  27 us
    pallas_call x1, Pallas kernels, body(): pl.pallas_call(functools.partial(return_kernel, n), out_shape=shape((rows...  16.8 us
    pallas_call x1, Pallas kernels, body(): pl.pallas_call(functools.partial(pack_kernel, n, geom), out_shape=(shape(...  3.64 us

profile of v1, /device:TPU:5, one launch (start us, length us, event | category | flops | bytes accessed | tf_op | source)
XLA Modules:
  0.0 121.0 jit_solution(17422441337709940095)
XLA Ops:
  0.6 3.6 %pack.1 = (bf16[18,32,128]{2,1,0:T(8,128)(2,1)}, s32[18,1,128]{2,1,0:T(1,128)}, bf16[4,384,512]{2,1,0:T(8,128)(2,1)}) custom-call(bf16[128,128]{1,0:T(8,128)(2,1)} %res_ref.1, s32[16]{0:T(128)} %chosen_ref.1, s32[4,128]{1,0:T(4,128)} %bitcast.4, s32[4,128]{1,0:T(4,128)} %bitcast.6, f32[4,384,512]{2,1,0:T(8,128)} %speed.1), custom_call_target="tpu_custom_call" | custom-call | tf_op jit(solution)/shard_map/pack/pallas_call | solution.py:317
  4.3 27.0 %exchange.1 = (bf16[16,3,32,128]{3,2,1,0:T(8,128)(2,1)}, s32[16,3,1,128]{3,2,1,0:T(1,128)}, bf16[2,3,384,512]{3,2,1,0:T(8,128)(2,1)}) custom-call(bf16[18,32,128]{2,1,0:T(8,128)(2,1)} %get-tuple-element.10.pay, s32[18,1,128]{2,1,0:T(1,128)} %get-tuple-element.11.cod, bf16[4,384,512]{2,1,0:T(8,128)(2,1)} %get-tuple-element.12.sp), custom_call_target="tpu_custom_call" | custom-call | tf_op jit(solution)/shard_map/exchange/pallas_call | solution.py:329
  31.3 71.5 %field.1 = (f32[4,384,512]{2,1,0:T(8,128)}, f32[16,32,128]{2,1,0:T(8,128)}) custom-call(bf16[16,3,32,128]{3,2,1,0:T(8,128)(2,1)} %get-tuple-element.13.got, s32[48,128]{1,0:T(8,128)} %bitcast.3, f32[128,128]{1,0:T(8,128)} %interp.3, f32[4,384,512]{2,1,0:T(8,128)} %speed.1, bf16[2,3,384,512]{3,2,1,0:T(8,128)(2,1)} %get-tuple-element.15.halo), custom_call_target="tpu_custom_call" | custom-call | tf_op jit(solution)/shard_map/field/pallas_call | solution.py:345
  102.8 16.8 %give_back.1 = f32[128,128]{1,0:T(8,128)} custom-call(f32[16,32,128]{2,1,0:T(8,128)} %get-tuple-element.17.sampled, s32[4,128]{1,0:T(4,128)} %bitcast.5, f32[128,128]{1,0:T(8,128)} %interp.3), custom_call_target="tpu_custom_call" | custom-call | tf_op jit(solution)/shard_map/give_back/pallas_call | solution.py:356
  119.6 1.5 %copy.9 = f32[128,128]{1,0:T(8,128)} copy(f32[128,128]{1,0:T(8,128)} %give_back.1) | data formatting | bytes 131072

commit v2 on v1

--- a/solution.py
+++ b/solution.py
@@ -29,6 +29,10 @@
 
 def dot32(a, b):
     return lax.dot_general(a, b, (((1,), (0,)), ((), ())), preferred_element_type=F32)
+
+
+def plane_rows(geom):
+    return 3 * geom[0] * (geom[1] + 8) + 8
 
 
 def slot_rows(dest, tiles):
@@ -64,8 +68,7 @@
     in_layer = block - layer * per_layer
     y = in_layer // nzb
     zb = in_layer - y * nzb
-    strip = layer * (ny // 8 + 1) + 1 + y // 8
-    flat = (strip * nzb + zb) * 8 + (y - y // 8 * 8)
+    flat = zb * plane_rows(geom) + layer * (ny + 8) + 8 + y
     hi = (flat // 64).astype(F32)
     lo = (flat - flat // 64 * 64).astype(F32)
     slots = slot_rows(ft_ref[...], tiles)
@@ -196,23 +199,28 @@
 def field_kernel(geom, got, codes, interp, speed, halo, field, sampled, ua, ub, vals):
     cx, ny, nz = geom
     nzb = nz // 128
-    tile = nzb * 8
-    strips = ny // 8
-    pitch = strips + 1
+    pitch = ny + 8
+    plane = plane_rows(geom)
     n = got.shape[0]
     span = 3 * CAP
     layers = 3 * cx
-    per_tile = cx * pitch * tile
+    per_tile = cx * pitch
     vals[...] = jnp.dot(got[...].reshape(n * span, 128).astype(F32), interp[...], precision=HIGH)
 
-    zero = jnp.zeros((tile, 128), F32)
-
-    @pl.loop(0, layers * pitch + 1, unroll=4)
+    zero = jnp.zeros((8, 128), F32)
+
+    @pl.loop(0, nzb * plane // 8 // 19)
     def _(s):
-        ua[pl.ds(pl.multiple_of(s * tile, tile), tile)] = zero
-
-    for l in range(layers + 1):
-        ub[l * pitch * tile : l * pitch * tile + tile] = zero
+        for i in range(19):
+            ua[pl.ds(pl.multiple_of(s * 152 + i * 8, 8), 8)] = zero
+
+    for row in range(nzb * plane // 152 * 152, nzb * plane, 8):
+        ua[row : row + 8] = zero
+
+    for zb in range(nzb):
+        for l in range(layers + 1):
+            row = zb * plane + l * pitch
+            ub[row : row + 8] = zero
 
     @pl.loop(0, n)
     def _(s):
@@ -221,38 +229,35 @@
                 at = codes[s * 3 + o, j] + o * per_tile
                 ua[pl.ds(at, 1)] = ua[pl.ds(at, 1)] + vals[pl.ds(s * span + o * CAP + j, 1)]
 
-    sub = iota((8, 128), 0)
     lane = iota((8, 128), 1)
-    first_sub, last_sub = sub == 0, sub == 7
     first_lane, last_lane = lane == 0, lane == 127
+    strips = next(k for k in (6, 4, 2) if ny % (8 * k) == 0)
 
     def layer_step(src, dst, l, rate_of, final):
-        @pl.loop(0, strips // 2)
+        @pl.loop(0, ny // (8 * strips))
         def _(p):
-            rates = [rate_of(p, zb) for zb in range(nzb)]
-            for h in range(2):
-                base = pl.multiple_of((l * pitch + 1 + p * 2 + h) * tile, tile)
-                centre = [src[pl.ds(base + zb * 8, 8)] for zb in range(nzb)]
+            rates = [rate_of(pl.multiple_of(p * 8 * strips, 16), zb, 8 * strips) for zb in range(nzb)]
+            for h in range(strips):
+                row = pl.multiple_of(p * 8 * strips + h * 8, 8)
+                base = pl.multiple_of(l * pitch + 8 + row, 8)
+                centre = [src[pl.ds(base + zb * plane, 8)] for zb in range(nzb)]
                 for zb in range(nzb):
                     c = centre[zb]
-                    before = src[pl.ds(base - tile + zb * 8, 8)]
-                    after = src[pl.ds(base + tile + zb * 8, 8)]
+                    at = base + zb * plane
                     left = centre[zb - 1] if zb > 0 else 0.0
                     right = centre[zb + 1] if zb + 1 < nzb else 0.0
-                    total = src[pl.ds(base - pitch * tile + zb * 8, 8)] + src[pl.ds(base + pitch * tile + zb * 8, 8)]
-                    total = total + pltpu.roll(jnp.where(last_sub, before, c), 1, 0)
-                    total = total + pltpu.roll(jnp.where(first_sub, after, c), 7, 0)
+                    total = src[pl.ds(at - pitch, 8)] + src[pl.ds(at + pitch, 8)]
+                    total = total + (src[pl.ds(at - 1, 8)] + src[pl.ds(at + 1, 8)])
                     total = total + pltpu.roll(jnp.where(last_lane, left, c), 1, 1)
                     total = total + pltpu.roll(jnp.where(first_lane, right, c), 127, 1)
                     new = c + rates[zb][h * 8 : h * 8 + 8] * (total - 6.0 * c)
-                    dst[pl.ds(base + zb * 8, 8)] = new
+                    dst[pl.ds(at, 8)] = new
                     if final is not None:
-                        field[final, pl.ds(pl.multiple_of(p * 16 + h * 8, 8), 8), zb * 128 : zb * 128 + 128] = new
+                        field[final, pl.ds(row, 8), zb * 128 : zb * 128 + 128] = new
 
     def rate_from(ref, index):
-        def rate_of(p, zb):
-            rows = pl.ds(pl.multiple_of(p * 16, 16), 16)
-            return RATE * ref[(*index, rows, slice(zb * 128, zb * 128 + 128))].astype(F32)
+        def rate_of(row, zb, size):
+            return RATE * ref[(*index, pl.ds(row, size), slice(zb * 128, zb * 128 + 128))].astype(F32)
         return rate_of
 
     src, dst = ua, ub
@@ -341,7 +346,7 @@
         compiler_params=pltpu.CompilerParams(collective_id=0, has_side_effects=True),
         name="exchange",
     )(pay, cod, sp)
-    flat = (3 * cx * (ny // 8 + 1) + 1) * (nz // 16)
+    flat = plane_rows(geom) * (nz // 128)
     field, sampled = pl.pallas_call(
         functools.partial(field_kernel, geom),
         out_shape=(shape(geom, F32), shape((n, CAP, samp), F32)),

time: 121 us -> 89.7 us (0.74)
  Pallas kernels: 119 us -> 87.4 us
    pallas_call x1, Pallas kernels: 71.5 us -> 39.9 us  [body(): pl.pallas_call(functools.partial(field_kernel, geom), out_shape=(shape(ge...]
where the time goes in v2:
time: 89.7 us; the launch traced here: 89.5 us
  Pallas kernels  87.4 us (97%)
  local copies, waits for them, and re-layouts  1.47 us (2%)
    pallas_call x1, Pallas kernels, body(): pl.pallas_call(functools.partial(field_kernel, geom), out_shape=(shape(ge...  39.9 us
    pallas_call x1, Pallas kernels, body(): pl.pallas_call(functools.partial(send_kernel, n, groups), out_shape=(shap...  27 us
    pallas_call x1, Pallas kernels, body(): pl.pallas_call(functools.partial(return_kernel, n), out_shape=shape((rows...  16.8 us
    pallas_call x1, Pallas kernels, body(): pl.pallas_call(functools.partial(pack_kernel, n, geom), out_shape=(shape(...  3.64 us

profile of v2, /device:TPU:5, one launch (start us, length us, event | category | flops | bytes accessed | tf_op | source)
XLA Modules:
  0.0 89.5 jit_solution(1202864759583499364)
XLA Ops:
  0.6 3.6 %pack.1 = (bf16[18,32,128]{2,1,0:T(8,128)(2,1)}, s32[18,1,128]{2,1,0:T(1,128)}, bf16[4,384,512]{2,1,0:T(8,128)(2,1)}) custom-call(bf16[128,128]{1,0:T(8,128)(2,1)} %res_ref.1, s32[16]{0:T(128)} %chosen_ref.1, s32[4,128]{1,0:T(4,128)} %bitcast.4, s32[4,128]{1,0:T(4,128)} %bitcast.6, f32[4,384,512]{2,1,0:T(8,128)} %speed.1), custom_call_target="tpu_custom_call" | custom-call | tf_op jit(solution)/shard_map/pack/pallas_call | solution.py:322
  4.3 27.0 %exchange.1 = (bf16[16,3,32,128]{3,2,1,0:T(8,128)(2,1)}, s32[16,3,1,128]{3,2,1,0:T(1,128)}, bf16[2,3,384,512]{3,2,1,0:T(8,128)(2,1)}) custom-call(bf16[18,32,128]{2,1,0:T(8,128)(2,1)} %get-tuple-element.10.pay, s32[18,1,128]{2,1,0:T(1,128)} %get-tuple-element.11.cod, bf16[4,384,512]{2,1,0:T(8,128)(2,1)} %get-tuple-element.12.sp), custom_call_target="tpu_custom_call" | custom-call | tf_op jit(solution)/shard_map/exchange/pallas_call | solution.py:334
  31.3 39.9 %field.1 = (f32[4,384,512]{2,1,0:T(8,128)}, f32[16,32,128]{2,1,0:T(8,128)}) custom-call(bf16[16,3,32,128]{3,2,1,0:T(8,128)(2,1)} %get-tuple-element.13.got, s32[48,128]{1,0:T(8,128)} %bitcast.3, f32[128,128]{1,0:T(8,128)} %interp.3, f32[4,384,512]{2,1,0:T(8,128)} %speed.1, bf16[2,3,384,512]{3,2,1,0:T(8,128)(2,1)} %get-tuple-element.15.halo), custom_call_target="tpu_custom_call" | custom-call | tf_op jit(solution)/shard_map/field/pallas_call | solution.py:350
  71.3 16.8 %give_back.1 = f32[128,128]{1,0:T(8,128)} custom-call(f32[16,32,128]{2,1,0:T(8,128)} %get-tuple-element.17.sampled, s32[4,128]{1,0:T(4,128)} %bitcast.5, f32[128,128]{1,0:T(8,128)} %interp.3), custom_call_target="tpu_custom_call" | custom-call | tf_op jit(solution)/shard_map/give_back/pallas_call | solution.py:361
  88.0 1.5 %copy.9 = f32[128,128]{1,0:T(8,128)} copy(f32[128,128]{1,0:T(8,128)} %give_back.1) | data formatting | bytes 131072

commit v3 on v2

--- a/solution.py
+++ b/solution.py
@@ -13,6 +13,7 @@
 HALO = STEPS - 1
 MESH = pl.DeviceIdType.MESH
 VMEM = pl.BlockSpec(memory_space=pltpu.VMEM)
+ANY = pl.BlockSpec(memory_space=pl.ANY)
 SMEM = pl.BlockSpec(memory_space=pltpu.SMEM)
 F32 = jnp.float32
 BF16 = jnp.bfloat16
@@ -121,16 +122,20 @@
     nb = me + 2 * odd - 1
     cb = me + 1 - 2 * odd
     inter = jnp.logical_and(nb >= 0, nb < n)
-    window = pl.ds(start, rows)
-
-    def piece(j):
+    cuts = isem.shape[1] // HALO
+
+    def window(i):
+        return pl.ds(start + i % cuts * (rows // cuts), rows // cuts)
+
+    def piece(i):
         return pltpu.make_async_remote_copy(
-            sp.at[odd + j, window], halo.at[1 - odd, j, window], isem.at[0, j], isem.at[1, j],
+            sp.at[odd + i // cuts, window(i)], halo.at[1 - odd, i // cuts, window(i)], isem.at[0, i], isem.at[1, i],
             device_id={"tile": nb}, device_id_type=MESH)
 
-    def forward(j):
+    def forward(i):
+        here = halo.at[odd, i // cuts, window(i)]
         return pltpu.make_async_remote_copy(
-            halo.at[odd, j, window], halo.at[odd, j, window], fsem.at[0, j], fsem.at[1, j],
+            here, here, fsem.at[0, i], fsem.at[1, i],
             device_id={"group": partner}, device_id_type=MESH)
 
     inside = pltpu.make_async_remote_copy(
@@ -139,7 +144,7 @@
 
     @pl.when(inter)
     def _():
-        for j in range(HALO):
+        for j in range(HALO * cuts):
             piece(j).start()
 
     inside.start()
@@ -166,23 +171,19 @@
     own.start()
     ownc.start()
 
-    @pl.when(jnp.logical_not(inter))
-    def _():
-        halo[odd] = jnp.zeros(halo.shape[1:], halo.dtype)
-
     if paired:
         @pl.when(inter)
         def _():
-            for j in range(HALO):
+            for j in range(HALO * cuts):
                 piece(j).wait_recv()
                 forward(j).start()
-            for j in range(HALO):
+            for j in range(HALO * cuts):
                 piece(j).wait_send()
                 forward(j).wait()
     else:
         @pl.when(inter)
         def _():
-            for j in range(HALO):
+            for j in range(HALO * cuts):
                 piece(j).wait()
 
     inside.wait()
@@ -196,7 +197,9 @@
     ownc.wait()
 
 
-def field_kernel(geom, got, codes, interp, speed, halo, field, sampled, ua, ub, vals):
+def field_kernel(
+    geom, got, codes, interp, speed_in, halo_in, field, sampled, ua, ub, vals, speed, halo, made, in_sem, out_sem
+):
     cx, ny, nz = geom
     nzb = nz // 128
     pitch = ny + 8
@@ -205,6 +208,20 @@
     span = 3 * CAP
     layers = 3 * cx
     per_tile = cx * pitch
+    me = lax.axis_index("tile")
+    own = pltpu.make_async_copy(speed_in, speed, in_sem.at[2])
+    own.start()
+    for side, there in ((0, me > 0), (1, me < n - 1)):
+        beside = pltpu.make_async_copy(halo_in.at[side], halo.at[side], in_sem.at[side])
+
+        @pl.when(there)
+        def _():
+            beside.start()
+
+        @pl.when(jnp.logical_not(there))
+        def _():
+            halo[side] = jnp.zeros(halo.shape[1:], halo.dtype)
+
     vals[...] = jnp.dot(got[...].reshape(n * span, 128).astype(F32), interp[...], precision=HIGH)
 
     zero = jnp.zeros((8, 128), F32)
@@ -231,46 +248,65 @@
 
     lane = iota((8, 128), 1)
     first_lane, last_lane = lane == 0, lane == 127
-    strips = next(k for k in (6, 4, 2) if ny % (8 * k) == 0)
-
-    def layer_step(src, dst, l, rate_of, final):
-        @pl.loop(0, ny // (8 * strips))
-        def _(p):
-            rates = [rate_of(pl.multiple_of(p * 8 * strips, 16), zb, 8 * strips) for zb in range(nzb)]
-            for h in range(strips):
-                row = pl.multiple_of(p * 8 * strips + h * 8, 8)
-                base = pl.multiple_of(l * pitch + 8 + row, 8)
-                centre = [src[pl.ds(base + zb * plane, 8)] for zb in range(nzb)]
+    def rate_at(l, row, zb):
+        at = (0, l - (cx - HALO)) if l < cx else (1, l - 2 * cx)
+        return RATE * halo[(*at, pl.ds(row, 16), slice(zb * 128, zb * 128 + 128))].astype(F32)
+
+    def step_rows(src, dst, first, last, row, final):
+        rates = {}
+        for h in range(2):
+            base = pl.multiple_of(row + 8 + h * 8, 8)
+
+            def strip(l):
+                return [src[pl.ds(base + l * pitch + zb * plane, 8)] for zb in range(nzb)]
+
+            below, here = strip(first - 1), strip(first)
+            for l in range(first, last):
+                above = strip(l + 1)
                 for zb in range(nzb):
-                    c = centre[zb]
-                    at = base + zb * plane
-                    left = centre[zb - 1] if zb > 0 else 0.0
-                    right = centre[zb + 1] if zb + 1 < nzb else 0.0
-                    total = src[pl.ds(at - pitch, 8)] + src[pl.ds(at + pitch, 8)]
+                    if h == 0 and (l < cx or l >= 2 * cx):
+                        rates[l, zb] = rate_at(l, row, zb)
+                    c = here[zb]
+                    at = base + l * pitch + zb * plane
+                    left = here[zb - 1] if zb > 0 else 0.0
+                    right = here[zb + 1] if zb + 1 < nzb else 0.0
+                    total = below[zb] + above[zb]
                     total = total + (src[pl.ds(at - 1, 8)] + src[pl.ds(at + 1, 8)])
                     total = total + pltpu.roll(jnp.where(last_lane, left, c), 1, 1)
                     total = total + pltpu.roll(jnp.where(first_lane, right, c), 127, 1)
-                    new = c + rates[zb][h * 8 : h * 8 + 8] * (total - 6.0 * c)
+                    rate = rates[l, zb][h * 8 : h * 8 + 8] if l < cx or l >= 2 * cx else RATE * speed[l - cx, pl.ds(row + h * 8, 8), zb * 128 : zb * 128 + 128]
+                    new = c + rate * (total - 6.0 * c)
                     dst[pl.ds(at, 8)] = new
-                    if final is not None:
-                        field[final, pl.ds(row, 8), zb * 128 : zb * 128 + 128] = new
-
-    def rate_from(ref, index):
-        def rate_of(row, zb, size):
-            return RATE * ref[(*index, pl.ds(row, size), slice(zb * 128, zb * 128 + 128))].astype(F32)
-        return rate_of
+                    if final:
+                        made[l - cx, pl.ds(row + h * 8, 8), zb * 128 : zb * 128 + 128] = new
+                below, here = here, above
+
+    own.wait()
+    for side, there in ((0, me > 0), (1, me < n - 1)):
+        @pl.when(there)
+        def _():
+            pltpu.make_async_copy(halo_in.at[side], halo.at[side], in_sem.at[side]).wait()
 
     src, dst = ua, ub
+    parts = out_sem.shape[0]
+    size = ny // parts
+
+    def give(part):
+        rows = pl.ds(part * size, size)
+        return pltpu.make_async_copy(made.at[:, rows], field.at[:, rows], out_sem.at[part])
+
     for step in range(STEPS):
         reach = STEPS - 1 - step
-        for l in range(cx - reach, 2 * cx + reach):
-            if l < cx:
-                rate_of = rate_from(halo, (0, l - (cx - HALO)))
-            elif l >= 2 * cx:
-                rate_of = rate_from(halo, (1, l - 2 * cx))
-            else:
-                rate_of = rate_from(speed, (l - cx,))
-            layer_step(src, dst, l, rate_of, l - cx if step == STEPS - 1 else None)
+        final = step == STEPS - 1
+        for part in range(parts if final else 1):
+            start, stop = (part * size, part * size + size) if final else (0, ny)
+
+            @pl.loop(start // 16, stop // 16)
+            def _(p):
+                step_rows(src, dst, cx - reach, 2 * cx + reach, pl.multiple_of(p * 16, 16), final)
+
+            if final:
+                give(part).start()
         src, dst = dst, src
 
     @pl.loop(0, n)
@@ -278,6 +314,9 @@
         for j in range(CAP):
             at = codes[s * 3 + 1, j] + per_tile
             sampled[s, pl.ds(j, 1)] = src[pl.ds(at, 1)]
+
+    for part in range(parts):
+        give(part).wait()
 
 
 def return_kernel(n, sampled, ft, interp, out, ret, sems, lsem):
@@ -338,10 +377,10 @@
             shape((n, 3, 1, 128), jnp.int32),
             shape((2, HALO, ny, nz), BF16),
         ),
-        in_specs=[VMEM] * 3,
-        out_specs=(VMEM,) * 3,
+        in_specs=[VMEM, VMEM, ANY],
+        out_specs=(VMEM, VMEM, ANY),
         scratch_shapes=[
-            dma((2, n)), dma((2, n)), dma((2, HALO)), dma((2, HALO)), dma((2,)), dma((2,)),
+            dma((2, n)), dma((2, n)), dma((2, 2 * HALO)), dma((2, 2 * HALO)), dma((2,)), dma((2,)),
         ],
         compiler_params=pltpu.CompilerParams(collective_id=0, has_side_effects=True),
         name="exchange",
@@ -350,11 +389,12 @@
     field, sampled = pl.pallas_call(
         functools.partial(field_kernel, geom),
         out_shape=(shape(geom, F32), shape((n, CAP, samp), F32)),
-        in_specs=[VMEM, SMEM, VMEM, VMEM, VMEM],
-        out_specs=(VMEM, VMEM),
+        in_specs=[VMEM, SMEM, VMEM, ANY, ANY],
+        out_specs=(ANY, VMEM),
         scratch_shapes=[
             pltpu.VMEM((flat, 128), F32), pltpu.VMEM((flat, 128), F32),
-            pltpu.VMEM((n * 3 * CAP, 128), F32),
+            pltpu.VMEM((n * 3 * CAP, 128), F32), pltpu.VMEM(geom, F32),
+            pltpu.VMEM((2, HALO, ny, nz), BF16), pltpu.VMEM(geom, F32), dma((3,)), dma((3,)),
         ],
         name="field",
     )(got, gotc.reshape(n * 3, 128), interp, speed, halo)

time: 89.7 us -> 77.9 us (0.87)
  Pallas kernels: 87.4 us -> 75.5 us
    pallas_call x1, Pallas kernels: 39.9 us -> 29.7 us  [body(): pl.pallas_call(functools.partial(field_kernel, geom), out_shape=(shape(ge...]
    pallas_call x1, Pallas kernels: 16.8 us -> 15.8 us  [body(): pl.pallas_call(functools.partial(return_kernel, n), out_shape=shape((rows...]
where the time goes in v3:
time: 77.9 us; the launch traced here: 77.7 us
  Pallas kernels  75.5 us (97%)
  local copies, waits for them, and re-layouts  1.47 us (2%)
    pallas_call x1, Pallas kernels, body(): pl.pallas_call(functools.partial(field_kernel, geom), out_shape=(shape(ge...  29.7 us
    pallas_call x1, Pallas kernels, body(): pl.pallas_call(functools.partial(send_kernel, n, groups), out_shape=(shap...  26.4 us
    pallas_call x1, Pallas kernels, body(): pl.pallas_call(functools.partial(return_kernel, n), out_shape=shape((rows...  15.8 us
    pallas_call x1, Pallas kernels, body(): pl.pallas_call(functools.partial(pack_kernel, n, geom), out_shape=(shape(...  3.64 us

profile of v3, /device:TPU:5, one launch (start us, length us, event | category | flops | bytes accessed | tf_op | source)
XLA Modules:
  0.0 77.7 jit_solution(5627822192992406027)
XLA Ops:
  0.6 3.6 %pack.1 = (bf16[18,32,128]{2,1,0:T(8,128)(2,1)}, s32[18,1,128]{2,1,0:T(1,128)}, bf16[4,384,512]{2,1,0:T(8,128)(2,1)}) custom-call(bf16[128,128]{1,0:T(8,128)(2,1)} %res_ref.1, s32[16]{0:T(128)} %chosen_ref.1, s32[4,128]{1,0:T(4,128)} %bitcast.4, s32[4,128]{1,0:T(4,128)} %bitcast.6, f32[4,384,512]{2,1,0:T(8,128)} %speed_in.1), custom_call_target="tpu_custom_call" | custom-call | tf_op jit(solution)/shard_map/pack/pallas_call | solution.py:361
  4.3 26.4 %exchange.1 = (bf16[16,3,32,128]{3,2,1,0:T(8,128)(2,1)}, s32[16,3,1,128]{3,2,1,0:T(1,128)}, bf16[2,3,384,512]{3,2,1,0:T(8,128)(2,1)}) custom-call(bf16[18,32,128]{2,1,0:T(8,128)(2,1)} %get-tuple-element.10.pay, s32[18,1,128]{2,1,0:T(1,128)} %get-tuple-element.11.cod, bf16[4,384,512]{2,1,0:T(8,128)(2,1)} %get-tuple-element.12.sp), custom_call_target="tpu_custom_call" | custom-call | tf_op jit(solution)/shard_map/exchange/pallas_call | solution.py:373
  30.6 29.7 %field.1 = (f32[4,384,512]{2,1,0:T(8,128)}, f32[16,32,128]{2,1,0:T(8,128)}) custom-call(bf16[16,3,32,128]{3,2,1,0:T(8,128)(2,1)} %get-tuple-element.13.got, s32[48,128]{1,0:T(8,128)} %bitcast.3, f32[128,128]{1,0:T(8,128)} %interp.3, f32[4,384,512]{2,1,0:T(8,128)} %speed_in.1, bf16[2,3,384,512]{3,2,1,0:T(8,128)(2,1)} %get-tuple-element.15.halo_in), custom_call_target="tpu_custom_call" | custom-call | tf_op jit(solution)/shard_map/field/pallas_call | solution.py:389
  60.4 15.8 %give_back.1 = f32[128,128]{1,0:T(8,128)} custom-call(f32[16,32,128]{2,1,0:T(8,128)} %get-tuple-element.17.sampled, s32[4,128]{1,0:T(4,128)} %bitcast.5, f32[128,128]{1,0:T(8,128)} %interp.3), custom_call_target="tpu_custom_call" | custom-call | tf_op jit(solution)/shard_map/give_back/pallas_call | solution.py:401
  76.2 1.5 %copy.9 = f32[128,128]{1,0:T(8,128)} copy(f32[128,128]{1,0:T(8,128)} %give_back.1) | data formatting | bytes 131072

commit v4 on v3

--- a/solution.py
+++ b/solution.py
@@ -51,8 +51,18 @@
     return out
 
 
-def pack_kernel(tiles, geom, res_ref, chosen_ref, ft_ref, fb_ref, speed_ref, pay_ref, cod_ref, sp_ref):
+def pack_kernel(tiles, geom, res_ref, chosen_ref, ft_ref, fb_ref, speed_in, pay_ref, cod_ref, sp_out,
+                speed_ref, sp_ref, in_sem, out_sem):
     cx, ny, nz = geom
+
+    def take(l):
+        return pltpu.make_async_copy(speed_in.at[l], speed_ref.at[l], in_sem.at[l])
+
+    def give(l):
+        return pltpu.make_async_copy(sp_ref.at[l], sp_out.at[l], out_sem.at[l])
+
+    for l in range(cx):
+        take(l).start()
     nzb = nz // 128
     per_layer = ny * nzb
     top, rows = ft_ref.shape
@@ -91,7 +101,11 @@
     for d in range(tiles):
         cod_ref[1 + d] = codes[d : d + 1]
     for l in range(cx):
+        take(l).wait()
         sp_ref[l] = speed_ref[l].astype(BF16)
+        give(l).start()
+    for l in range(cx):
+        give(l).wait()
 
 
 def greet(n, me, partner=None):
@@ -319,7 +333,7 @@
         give(part).wait()
 
 
-def return_kernel(n, sampled, ft, interp, out, ret, sems, lsem):
+def return_kernel(n, sampled, ft, out, ret, sems, lsem):
     me = lax.axis_index("tile")
     greet(n, me)
 
@@ -345,11 +359,9 @@
     def _(i):
         block(i).wait()
 
-    total = lax.dot_general(
+    out[...] = lax.dot_general(
         place, ret[...].reshape(n * CAP, 128), (((0,), (0,)), ((), ())),
         precision=HIGH, preferred_element_type=F32)
-    out[...] = lax.dot_general(
-        total, interp[...], (((1,), (1,)), ((), ())), precision=HIGH, preferred_element_type=F32)
 
 
 def body(groups, residual, chosen, footprint_tile, footprint_block, interp, speed):
@@ -357,6 +369,7 @@
     cx, ny, nz = geom = speed.shape
     rows, samp = residual.shape
     shape = jax.ShapeDtypeStruct
+    dma = pltpu.SemaphoreType.DMA
     ft, fb = footprint_tile.T, footprint_block.T
     pay, cod, sp = pl.pallas_call(
         functools.partial(pack_kernel, n, geom),
@@ -365,11 +378,11 @@
             shape((n + 2, 1, 128), jnp.int32),
             shape(geom, BF16),
         ),
-        in_specs=[VMEM, SMEM, VMEM, VMEM, VMEM],
-        out_specs=(VMEM, VMEM, VMEM),
+        in_specs=[VMEM, SMEM, VMEM, VMEM, ANY],
+        out_specs=(VMEM, VMEM, ANY),
+        scratch_shapes=[pltpu.VMEM(geom, F32), pltpu.VMEM(geom, BF16), dma((cx,)), dma((cx,))],
         name="pack",
     )(residual, chosen, ft, fb, speed)
-    dma = pltpu.SemaphoreType.DMA
     got, gotc, halo = pl.pallas_call(
         functools.partial(send_kernel, n, groups),
         out_shape=(
@@ -398,16 +411,16 @@
         ],
         name="field",
     )(got, gotc.reshape(n * 3, 128), interp, speed, halo)
-    partials = pl.pallas_call(
+    summed = pl.pallas_call(
         functools.partial(return_kernel, n),
         out_shape=shape((rows, samp), F32),
-        in_specs=[VMEM] * 3,
+        in_specs=[VMEM] * 2,
         out_specs=VMEM,
         scratch_shapes=[pltpu.VMEM((n, CAP, samp), F32), dma((2, n)), dma],
         compiler_params=pltpu.CompilerParams(collective_id=1, has_side_effects=True),
         name="give_back",
-    )(sampled, ft, interp)
-    return field, partials
+    )(sampled, ft)
+    return field, jnp.dot(summed, interp.T, precision=HIGH)
 
 
 def solution(mesh):

time: 77.9 us -> 78.5 us (level)
  matrix products: 0 us -> 1.74 us
  local copies, waits for them, and re-layouts: 1.47 us -> 0.01 us
    dot_general x0 -> x1, matrix products: none -> 1.74 us  [body(): return (field, jnp.dot(summed, interp.T, precision=HIGH))]
    unnamed x1 -> x2, local copies, waits for them, and re-layouts: 1.47 us -> 0.01 us
where the time goes in v4:
time: 78.5 us; the launch traced here: 78.2 us
  Pallas kernels  75.8 us (97%)
  matrix products  1.74 us (2%)
    pallas_call x1, Pallas kernels, body(): pl.pallas_call(functools.partial(field_kernel, geom), out_shape=(shape(ge...  29.8 us
    pallas_call x1, Pallas kernels, body(): pl.pallas_call(functools.partial(send_kernel, n, groups), out_shape=(shap...  26.4 us
    pallas_call x1, Pallas kernels, body(): pl.pallas_call(functools.partial(return_kernel, n), out_shape=shape((rows...  15.5 us
    pallas_call x1, Pallas kernels, body(): pl.pallas_call(functools.partial(pack_kernel, n, geom), out_shape=(shape(...  4.2 us
    dot_general x1, matrix products, body(): return (field, jnp.dot(summed, interp.T, precision=HIGH))  1.74 us

profile of v4, /device:TPU:5, one launch (start us, length us, event | category | flops | bytes accessed | tf_op | source)
XLA Modules:
  0.0 78.2 jit_solution(5777656549932131551)
XLA Ops:
  0.6 4.2 %pack.1 = (bf16[18,32,128]{2,1,0:T(8,128)(2,1)}, s32[18,1,128]{2,1,0:T(1,128)}, bf16[4,384,512]{2,1,0:T(8,128)(2,1)}) custom-call(bf16[128,128]{1,0:T(8,128)(2,1)} %res_ref.1, s32[16]{0:T(128)} %chosen_ref.1, s32[4,128]{1,0:T(4,128)} %bitcast.6, s32[4,128]{1,0:T(4,128)} %bitcast.8, f32[4,384,512]{2,1,0:T(8,128)} %speed_in.3), custom_call_target="tpu_custom_call" | custom-call | tf_op jit(solution)/shard_map/pack/pallas_call | solution.py:374
  4.8 26.4 %exchange.1 = (bf16[16,3,32,128]{3,2,1,0:T(8,128)(2,1)}, s32[16,3,1,128]{3,2,1,0:T(1,128)}, bf16[2,3,384,512]{3,2,1,0:T(8,128)(2,1)}) custom-call(bf16[18,32,128]{2,1,0:T(8,128)(2,1)} %get-tuple-element.10.pay, s32[18,1,128]{2,1,0:T(1,128)} %get-tuple-element.11.cod, bf16[4,384,512]{2,1,0:T(8,128)(2,1)} %get-tuple-element.12.sp), custom_call_target="tpu_custom_call" | custom-call | tf_op jit(solution)/shard_map/exchange/pallas_call | solution.py:386
  31.2 0.0 copy-start
  31.2 29.8 %field.1 = (f32[4,384,512]{2,1,0:T(8,128)}, f32[16,32,128]{2,1,0:T(8,128)}) custom-call(bf16[16,3,32,128]{3,2,1,0:T(8,128)(2,1)} %get-tuple-element.13.got, s32[48,128]{1,0:T(8,128)} %bitcast.5, f32[128,128]{1,0:T(8,128)} %interp.1, f32[4,384,512]{2,1,0:T(8,128)} %speed_in.3, bf16[2,3,384,512]{3,2,1,0:T(8,128)(2,1)} %get-tuple-element.15.halo_in), custom_call_target="tpu_custom_call" | custom-call | tf_op jit(solution)/shard_map/field/pallas_call | solution.py:402
  61.0 15.5 %give_back.1 = f32[128,128]{1,0:T(8,128)} custom-call(f32[16,32,128]{2,1,0:T(8,128)} %get-tuple-element.17.sampled, s32[4,128]{1,0:T(4,128)} %bitcast.7), custom_call_target="tpu_custom_call" | custom-call | tf_op jit(solution)/shard_map/give_back/pallas_call | solution.py:414
  76.5 0.0 copy-done
  76.5 1.7 %fusion = f32[128,128]{1,0:T(8,128)} fusion(f32[128,128]{1,0:T(8,128)} %give_back.1, f32[128,128]{1,0:T(8,128)S(1)} %copy-done), kind=kOutput, calls=%fused_computation | convolution fusion | flops 25165824 | bytes 196608 | tf_op jit(solution)/shard_map/dot_general | solution.py:423
Async XLA Ops:
  31.2 45.3 %copy-start = (f32[128,128]{1,0:T(8,128)S(1)}, f32[128,128]{1,0:T(8,128)}, u32[]{:S(2)}) copy-start(f32[128,128]{1,0:T(8,128)} %interp.1) | copy-start | bytes 196612
